TPU v7x, 32 devices: a whole 2x2x4 slice. The times are simulated.
32 devices in a mesh: gx: 4 (over z), gy: 4 (over x, core), gz: 2 (over y).
Axes of the slice: x: 2, y: 2, z: 4, core: 2. Of those that a mesh axis runs over, the one named last changes fastest.
Arguments:
- elevation: float32 [256, 8192], P('gx', ('gy', 'gz')), may hold values from -1 to 1
- surface_potential: float32 [256, 8192], P('gx', ('gy', 'gz')), may hold values from -2 to 2
- seabed: int32 [256, 8192], P('gx', 'gy'), may hold values from 384 to 1023
- interior_potential: float32 [16, 256, 8192], P('gz', 'gx', 'gy'), may hold values from -1.5 to 1.5
Outputs:
- new_elevation: float32 [256, 8192], P('gx', ('gy', 'gz'))
- new_potential: float32 [256, 8192], P('gx', ('gy', 'gz'))
- laplace_apply: float32 [16, 256, 8192], P('gz', 'gx', 'gy')
All inputs are finite; a program needn't handle non-finite values.
Results may differ from a plain program's by a relative error of at most 0.0003.
Values sent between devices are 32-bit elements; how exact they have to be, the bound alone decides.
No kernel may reach another device: no remote copies, remote signals or barrier semaphores. Data moves between devices by JAX's collectives and lax.ppermute only.
A program may use at most 64 MiB of HBM per device.

v0:
```python
import jax
import jax.numpy as jnp
from jax import lax
from jax.sharding import PartitionSpec as P

time_step = 0.05
depth_unit = 0.015625


def with_halo(block, sides, width):
    for axis, dim in sides:
        count = lax.axis_size(axis)
        forward = [(i, i + 1) for i in range(count - 1)]
        forward.append((count - 1, 0))
        backward = [(target, source) for source, target in forward]
        low = lax.ppermute(
            lax.slice_in_dim(block, block.shape[dim] - width, None, axis=dim), axis, forward
        )
        high = lax.ppermute(lax.slice_in_dim(block, 0, width, axis=dim), axis, backward)
        block = jnp.concatenate([low, block, high], axis=dim)
    return block


def partner_2(value, axis, bit):
    mask = 2**bit
    pairs = [(source, source ^ mask) for source in range(lax.axis_size(axis))]
    return lax.ppermute(value, axis, pairs)


def window(extended, step_north, step_east, margin):
    height = extended.shape[-2] - 2 * margin
    breadth = extended.shape[-1] - 2 * margin
    return extended[
        ...,
        margin + step_north : margin + step_north + height,
        margin + step_east : margin + step_east + breadth,
    ]


def rates(extended):
    grad_north = (
        8.0 * (window(extended, 1, 0, 2) - window(extended, -1, 0, 2))
        - (window(extended, 2, 0, 2) - window(extended, -2, 0, 2))
    ) / 12.0
    grad_east = (
        8.0 * (window(extended, 0, 1, 2) - window(extended, 0, -1, 2))
        - (window(extended, 0, 2, 2) - window(extended, 0, -2, 2))
    ) / 12.0
    centre = window(extended, 0, 0, 2)
    poten = extended[1]
    curve_north = (
        -window(poten, 2, 0, 2)
        + 16.0 * window(poten, 1, 0, 2)
        - 30.0 * centre[1]
        + 16.0 * window(poten, -1, 0, 2)
        - window(poten, -2, 0, 2)
    )
    curve_east = (
        -window(poten, 0, 2, 2)
        + 16.0 * window(poten, 0, 1, 2)
        - 30.0 * centre[1]
        + 16.0 * window(poten, 0, -1, 2)
        - window(poten, 0, -2, 2)
    )
    curvature = (curve_north + curve_east) / 12.0
    rate_height = curvature - (grad_north[0] * grad_north[1] + grad_east[0] * grad_east[1])
    rate_potential = -centre[0] - 0.5 * (
        grad_north[1] * grad_north[1] + grad_east[1] * grad_east[1]
    )
    return jnp.stack([rate_height, rate_potential])


def shards(elevation, surface_potential, seabed, interior_potential):
    surface_pair = jnp.stack([elevation, surface_potential])
    depth = seabed.astype(jnp.float32) * depth_unit
    layers = interior_potential.shape[0]
    surface_tile = lax.all_gather(surface_pair, "gz", axis=2, tiled=True)
    triple = jnp.concatenate([surface_tile, depth[None]], 0)
    deep_wide = with_halo(triple, (("gx", 1), ("gy", 2)), 5)
    start_pair = deep_wide[:2]
    section_one = start_pair[:, 2:-2, 2:-2] + time_step * rates(start_pair)
    surface_rim = 0.5 * (
        start_pair[:, 4:-4, 4:-4] + section_one[:, 2:-2, 2:-2] + time_step * rates(section_one)
    )
    depth_rim = deep_wide[2, 4:-4, 4:-4]
    plane_wide = jnp.stack([depth_rim + surface_rim[0], surface_rim[1], depth_rim])
    own_width = surface_pair.shape[2]
    updated = lax.dynamic_slice_in_dim(
        surface_rim[:, 1:-1, 1:-1], lax.axis_index("gz") * own_width, own_width, 2
    )
    volume_wide = with_halo(interior_potential, (("gx", 1), ("gy", 2)), 1)
    layer_group = lax.axis_index("gz")
    bottom_group = layer_group == 0
    outgoing = jnp.where(bottom_group, volume_wide[-1], volume_wide[0])
    partner = partner_2(outgoing, "gz", 0)
    ghost_below = jnp.where(bottom_group, volume_wide[0], partner)
    ghost_above = jnp.where(bottom_group, partner, 2.0 * plane_wide[1] - volume_wide[-1])
    column_stack = jnp.concatenate([ghost_below[None], volume_wide, ghost_above[None]], 0)
    column_centre = plane_wide[0, 1:-1, 1:-1]
    column_north = 0.5 * (plane_wide[0, 2:, 1:-1] - plane_wide[0, :-2, 1:-1])
    column_east = 0.5 * (plane_wide[0, 1:-1, 2:] - plane_wide[0, 1:-1, :-2])
    depth_north = 0.5 * (plane_wide[2, 2:, 1:-1] - plane_wide[2, :-2, 1:-1])
    depth_east = 0.5 * (plane_wide[2, 1:-1, 2:] - plane_wide[2, 1:-1, :-2])
    total_layers = layers * lax.axis_size("gz")
    sigma_level = (
        (layer_group * layers + jnp.arange(layers, dtype=jnp.int32)).astype(jnp.float32) + 0.5
    ) / total_layers
    sigma_level = sigma_level[:, None, None]
    slope_north = (depth_north - sigma_level * column_north) / column_centre
    slope_east = (depth_east - sigma_level * column_east) / column_centre
    spacing = 1.0 / total_layers
    middle_stack = column_stack[1:-1]
    upper_stack = column_stack[2:]
    lower_stack = column_stack[:-2]
    centre = middle_stack[:, 1:-1, 1:-1]
    second_north = middle_stack[:, 2:, 1:-1] - 2.0 * centre + middle_stack[:, :-2, 1:-1]
    second_east = middle_stack[:, 1:-1, 2:] - 2.0 * centre + middle_stack[:, 1:-1, :-2]
    mixed_north = (
        upper_stack[:, 2:, 1:-1]
        - upper_stack[:, :-2, 1:-1]
        - lower_stack[:, 2:, 1:-1]
        + lower_stack[:, :-2, 1:-1]
    ) / (4.0 * spacing)
    mixed_east = (
        upper_stack[:, 1:-1, 2:]
        - upper_stack[:, 1:-1, :-2]
        - lower_stack[:, 1:-1, 2:]
        + lower_stack[:, 1:-1, :-2]
    ) / (4.0 * spacing)
    vertical = (upper_stack[:, 1:-1, 1:-1] - 2.0 * centre + lower_stack[:, 1:-1, 1:-1]) / (
        spacing * spacing
    )
    weight = (
        slope_north * slope_north + slope_east * slope_east + 1.0 / (column_centre * column_centre)
    )
    laplace_apply = (
        second_north
        + second_east
        + 2.0 * slope_north * mixed_north
        + 2.0 * slope_east * mixed_east
        + weight * vertical
    )
    return (updated[0], updated[1], laplace_apply)


def solution(mesh):
    return jax.shard_map(
        shards,
        mesh=mesh,
        in_specs=(P("gx", ("gy", "gz")), P("gx", ("gy", "gz")), P("gx", "gy"), P("gz", "gx", "gy")),
        out_specs=(P("gx", ("gy", "gz")), P("gx", ("gy", "gz")), P("gz", "gx", "gy")),
        check_vma=False,
    )
```

profile of v0, /device:TPU:1, one launch (start us, length us, event | category | flops | bytes accessed | tf_op | source)
XLA Modules:
  0.0 121.5 jit_solution(9207310284389499734)
XLA Ops:
  7.2 1.9 %pad_maximum_fusion.24 = f32[2,64,1024]{2,1,0:T(8,128)} fusion(f32[1,64,1024]{2,1,0:T(8,128)} %bitcast.74, f32[1,64,1024]{2,1,0:T(8,128)} %bitcast.75), kind=kLoop, calls=%fused_computation.172 | loop fusion | flops 131072 | bytes 1048576 | tf_op jit(solution)/shard_map/stack | solution.py:74
  9.1 1.3 %fusion.87 = (f32[8,1,2048]{2,1,0:T(1,128)S(1)}, f32[8,1,2048]{2,1,0:T(1,128)S(1)}) fusion(f32[8,64,2048]{2,1,0:T(8,128)} %param.7), kind=kLoop, calls=%fused_computation.182 | loop fusion | bytes 262144 | tf_op jit(solution)/shard_map/slice | solution.py:17
  10.4 2.2 %collective-permute-start.5 = (f32[8,1,2048]{2,1,0:T(1,128)S(1)}, f32[8,1,2048]{2,1,0:T(1,128)S(1)}, u32[]{:S(2)}, u32[]{:S(2)}) collective-permute-start(f32[8,1,2048]{2,1,0:T(1,128)S(1)} %get-tuple-element.7), channel_id=1, source_target_pairs={{0,8},{8,16},{16,24},{24,0},{1,9},{9,17},{17,25},{25,1},{2,10},{10... | collective-permute-start | bytes 196616 | tf_op jit(solution)/shard_map/ppermute | solution.py:16
  12.6 2.1 %collective-permute-start.4 = (f32[8,1,2048]{2,1,0:T(1,128)S(1)}, f32[8,1,2048]{2,1,0:T(1,128)S(1)}, u32[]{:S(2)}, u32[]{:S(2)}) collective-permute-start(f32[8,1,2048]{2,1,0:T(1,128)S(1)} %get-tuple-element.8), channel_id=1, source_target_pairs={{8,0},{16,8},{24,16},{0,24},{9,1},{17,9},{25,17},{1,25},{10,2},{18... | collective-permute-start | bytes 196616 | tf_op jit(solution)/shard_map/ppermute | solution.py:19
  16.7 5.5 %pad_maximum_fusion = f32[8,66,2048]{2,1,0:T(8,128)} fusion(f32[8,1,2048]{2,1,0:T(1,128)S(1)} %collective-permute-done.4, f32[8,64,2048]{2,1,0:T(8,128)} %param.7, f32[8,1,2048]{2,1,0:T(1,128)S(1)} %collective-permute-done.5), kind=kLoop, calls=%fused_computation.16 | loop fusion | flops 2162688 | bytes 8650752 | tf_op jit(solution)/shard_map/concatenate | solution.py:20
  22.2 11.1 %all-gather.2.cloned.1.call-done = f32[2,64,2048]{2,1,0:T(8,128)} async-done(((f32[2,64,1024]{2,1,0:T(8,128)}), f32[2,64,2048]{2,1,0:T(8,128)}) %all-gather.2.cloned.1.call-update) | async-done | bytes 1048592 | tf_op jit(solution)/shard_map/all_gather | solution.py:77
  33.3 1.7 %pad_maximum_fusion.26 = (f32[3,5,2048]{2,1,0:T(8,128)}, f32[3,5,2048]{2,1,0:T(8,128)S(1)}) fusion(f32[1,64,2048]{2,1,0:T(8,128)S(1)} %multiply_bitcast_fusion, f32[2,64,2048]{2,1,0:T(8,128)} %all-gather.2.cloned.1.call-done), kind=kLoop, calls=%fused_computation.179 | loop fusion | flops 61440 | bytes 1818624 | tf_op jit(solution)/shard_map/slice | solution.py:17
  35.0 1.2 collective-permute-start
  36.2 2.1 %collective-permute-start.1 = (f32[3,5,2048]{2,1,0:T(8,128)S(1)}, f32[3,5,2048]{2,1,0:T(8,128)S(1)}, u32[]{:S(2)}, u32[]{:S(2)}) collective-permute-start(f32[3,5,2048]{2,1,0:T(8,128)S(1)} %get-tuple-element.16), channel_id=1, source_target_pairs={{8,0},{16,8},{24,16},{0,24},{9,1},{17,9},{25,17},{1,25},{10,2},{18... | collective-permute-start | bytes 368648 | tf_op jit(solution)/shard_map/ppermute | solution.py:19
  39.4 1.5 %collective-permute-start.6 = (f32[8,66,1]{2,1,0:T(8,128)S(1)}, f32[8,66,1]{2,1,0:T(8,128)S(1)}, u32[]{:S(2)}, u32[]{:S(2)}) collective-permute-start(f32[8,66,1]{2,1,0:T(8,128)S(1)} %get-tuple-element.5), channel_id=1, source_target_pairs={{2,0},{4,2},{6,4},{0,6},{3,1},{5,3},{7,5},{1,7},{10,8},{12,10},{14... | collective-permute-start | bytes 6344 | tf_op jit(solution)/shard_map/ppermute | solution.py:19
  42.6 7.1 %collective-permute-done.6 = f32[8,66,1]{2,1,0:T(8,128)S(1)} collective-permute-done((f32[8,66,1]{2,1,0:T(8,128)S(1)}, f32[8,66,1]{2,1,0:T(8,128)S(1)}, u32[]{:S(2)}, u32[]{:S(2)}) %collective-permute-start.6) | collective-permute-done | bytes 2144 | tf_op jit(solution)/shard_map/ppermute | solution.py:19
  49.7 7.0 %concatenate.56 = f32[8,66,2050]{2,1,0:T(8,128)} concatenate(f32[8,66,1]{2,1,0:T(8,128)S(1)} %collective-permute-done.7, f32[8,66,2048]{2,1,0:T(8,128)} %pad_maximum_fusion, f32[8,66,1]{2,1,0:T(8,128)S(1)} %collective-permute-done.6), dimensions={2} | concatenate | bytes 8659200 | tf_op jit(solution)/shard_map/concatenate | solution.py:20
  57.6 1.3 %collective-permute-start.2 = (f32[3,74,5]{2,1,0:T(8,128)S(1)}, f32[3,74,5]{2,1,0:T(8,128)}, u32[]{:S(2)}, u32[]{:S(2)}) collective-permute-start(f32[3,74,5]{2,1,0:T(8,128)S(1)} %get-tuple-element.14), channel_id=1, source_target_pairs={{0,2},{2,4},{4,6},{6,0},{1,3},{3,5},{5,7},{7,1},{8,10},{10,12},{12... | collective-permute-start | bytes 13328 | tf_op jit(solution)/shard_map/ppermute | solution.py:16
  58.9 2.2 %fusion.75 = f32[66,2050]{1,0:T(8,128)} fusion(f32[8,66,2050]{2,1,0:T(8,128)} %concatenate.56, pred[]{:T(512)S(6)} %eq.3), kind=kLoop, calls=%fused_computation.147 | loop fusion | flops 135300 | bytes 1623601 | tf_op jit(solution)/shard_map/jit(_where)/select_n | solution.py:94
  61.3 1.8 %collective-permute-done.3 = f32[3,74,5]{2,1,0:T(8,128)S(1)} collective-permute-done((f32[3,74,5]{2,1,0:T(8,128)S(1)}, f32[3,74,5]{2,1,0:T(8,128)S(1)}, u32[]{:S(2)}, u32[]{:S(2)}) %collective-permute-start.3) | collective-permute-done | bytes 4472 | tf_op jit(solution)/shard_map/ppermute | solution.py:19
  63.8 3.0 %concatenate.48 = f32[3,74,2058]{2,1,0:T(8,128)S(1)} concatenate(f32[3,74,5]{2,1,0:T(8,128)} %collective-permute-done.2, f32[3,74,2048]{2,1,0:T(8,128)} %copy-done.2, f32[3,74,5]{2,1,0:T(8,128)} %copy-done.7), dimensions={2} | concatenate | bytes 3655008 | tf_op jit(solution)/shard_map/concatenate | solution.py:20
  66.9 2.4 %fusion.41 = (f32[2,70,2054]{2,1,0:T(8,128)S(1)}, f32[2,70,2054]{2,1,0:T(8,128)S(1)}) fusion(f32[3,74,2058]{2,1,0:T(8,128)S(1)} %concatenate.48), kind=kLoop, calls=%fused_computation.78 | loop fusion | flops 2875600 | bytes 11502400 | tf_op jit(solution)/shard_map/div | solution.py:41
  69.6 1.4 %fusion.65 = f32[1,70,2054]{2,1,0:T(8,128)S(1)} fusion(f32[2,70,2054]{2,1,0:T(8,128)S(1)} %get-tuple-element.10, f32[2,70,2054]{2,1,0:T(8,128)S(1)} %get-tuple-element.9, f32[74,2058]{1,0:T(8,128)S(1)} %slice_bitcast_fusion, f32[3,74,2058]{2,1,0:T(8,128)S(1)} %concatenate.48), kind=kLoop, calls=%fused_computation.126 | loop fusion | flops 3019380 | bytes 8051680 | tf_op jit(solution)/shard_map/stack | solution.py:70
  71.4 2.4 %fusion.33 = (f32[2,66,2050]{2,1,0:T(8,128)S(1)}, f32[2,66,2050]{2,1,0:T(8,128)S(1)}) fusion(f32[2,70,2054]{2,1,0:T(8,128)S(1)} %slice_add_fusion.1), kind=kLoop, calls=%fused_computation.65 | loop fusion | flops 2706000 | bytes 10824000 | tf_op jit(solution)/shard_map/div | solution.py:41
  74.2 1.4 %fusion.51 = f32[1,66,2050]{2,1,0:T(8,128)S(1)} fusion(f32[2,66,2050]{2,1,0:T(8,128)S(1)} %get-tuple-element.18, f32[2,66,2050]{2,1,0:T(8,128)S(1)} %get-tuple-element.17, f32[70,2054]{1,0:T(8,128)S(1)} %slice_bitcast_fusion.3, f32[2,70,2054]{2,1,0:T(8,128)S(1)} %slice_add_fusion.1), kind=kLoop, calls=%fused_computation.99 | loop fusion | flops 2841300 | bytes 7576800 | tf_op jit(solution)/shard_map/stack | solution.py:70
  77.0 2.5 %fusion.85 = (f32[64,2048]{1,0:T(8,128)}, f32[64,2048]{1,0:T(8,128)}) fusion(f32[3,5,2048]{2,1,0:T(8,128)S(1)} %collective-permute-done, f32[1,64,2048]{2,1,0:T(8,128)S(1)} %copy-done.4, f32[2,64,2048]{2,1,0:T(8,128)S(1)} %copy-done.1, f32[3,5,2048]{2,1,0:T(8,128)S(1)} %collective-permute-done.1, f32[3,74,5]{2,1,0:T(8,128)} %collective-permute-done.2, ...), kind=kLoop, calls=%fused_computation.168 | loop fusion | flops 2097152 | bytes 2876080 | tf_op jit(solution)/shard_map/sub | solution.py:109
  80.2 2.0 %fusion.82 = (f32[64,2048]{1,0:T(8,128)}, f32[64,2048]{1,0:T(8,128)}, f32[64,2048]{1,0:T(8,128)}, f32[64,2048]{1,0:T(8,128)}) fusion(f32[1,66,2050]{2,1,0:T(8,128)S(1)} %slice_add_fusion.2), kind=kLoop, calls=%fused_computation.164 | loop fusion | flops 786432 | bytes 4718592 | tf_op jit(solution)/shard_map/mul | solution.py:109
  82.2 2.1 %fusion.46 = (f32[1,66,2050]{2,1,0:T(8,128)S(1)}, f32[1,66,2050]{2,1,0:T(8,128)}) fusion(f32[66,2050]{1,0:T(8,128)} %collective-permute-done.8, f32[2,66,2050]{2,1,0:T(8,128)S(1)} %fusion.36, f32[8,66,2050]{2,1,0:T(8,128)S(1)} %bitcast.73, pred[]{:T(512)S(6)} %eq.3), kind=kLoop, calls=%fused_computation.89 | loop fusion | flops 541200 | bytes 3247201 | tf_op jit(solution)/shard_map/broadcast_in_dim | solution.py:98
  84.3 30.3 %fusion.5 = f32[8,64,2048]{2,1,0:T(8,128)} fusion(f32[8,66,2050]{2,1,0:T(8,128)S(1)} %bitcast.73, f32[1,66,2050]{2,1,0:T(8,128)} %get-tuple-element.4, f32[1,66,2050]{2,1,0:T(8,128)S(1)} %get-tuple-element.3, f32[8,66,1]{2,1,0:T(8,128)} %copy-done.6, f32[8,1,2048]{2,1,0:T(1,128)} %copy-done.11, f32[8,64,2048]{2,1,0:T(8,128)S(1)} %copy-done, ...), kind=kLoop, calls=%fused_computation.22 | loop fusion | flops 55574528 | bytes 17081664 | tf_op jit(solution)/shard_map/add | solution.py:137
  (55 shorter events, 10.1 us)
Async XLA Ops:
  7.2 26.1 %all-gather.2.cloned.1.call-start = ((), (), s32[]{:S(2)}) async-start(), calls=%async_computation | async-start | bytes 1572864 | tf_op jit(solution)/shard_map/all_gather | solution.py:77
  10.4 5.9 %collective-permute-start.5 = (f32[8,1,2048]{2,1,0:T(1,128)S(1)}, f32[8,1,2048]{2,1,0:T(1,128)S(1)}, u32[]{:S(2)}, u32[]{:S(2)}) collective-permute-start(f32[8,1,2048]{2,1,0:T(1,128)S(1)} %get-tuple-element.7), channel_id=1, source_target_pairs={{0,8},{8,16},{16,24},{24,0},{1,9},{9,17},{17,25},{25,1},{2,10},{10... | collective-permute-start | bytes 196616 | tf_op jit(solution)/shard_map/ppermute | solution.py:16
  12.6 4.1 %collective-permute-start.4 = (f32[8,1,2048]{2,1,0:T(1,128)S(1)}, f32[8,1,2048]{2,1,0:T(1,128)S(1)}, u32[]{:S(2)}, u32[]{:S(2)}) collective-permute-start(f32[8,1,2048]{2,1,0:T(1,128)S(1)} %get-tuple-element.8), channel_id=1, source_target_pairs={{8,0},{16,8},{24,16},{0,24},{9,1},{17,9},{25,17},{1,25},{10,2},{18... | collective-permute-start | bytes 196616 | tf_op jit(solution)/shard_map/ppermute | solution.py:19
  15.8 40.9 %copy-start.3 = (f32[1,64,2048]{2,1,0:T(8,128)}, f32[1,64,2048]{2,1,0:T(8,128)S(1)}, u32[]{:S(2)}) copy-start(f32[1,64,2048]{2,1,0:T(8,128)S(1)} %multiply_bitcast_fusion) | copy-start | bytes 1572868
  16.4 5.8 %copy-start.9 = (f32[8,1,2048]{2,1,0:T(1,128)}, f32[8,1,2048]{2,1,0:T(1,128)S(1)}, u32[]{:S(2)}) copy-start(f32[8,1,2048]{2,1,0:T(1,128)S(1)} %collective-permute-done.5) | copy-start | bytes 196612
  16.7 5.5 %copy-start.11 = (f32[8,1,2048]{2,1,0:T(1,128)}, f32[8,1,2048]{2,1,0:T(1,128)S(1)}, u32[]{:S(2)}) copy-start(f32[8,1,2048]{2,1,0:T(1,128)S(1)} %collective-permute-done.4) | copy-start | bytes 196612
  35.0 21.7 %collective-permute-start = (f32[3,5,2048]{2,1,0:T(8,128)}, f32[3,5,2048]{2,1,0:T(8,128)S(1)}, u32[]{:S(2)}, u32[]{:S(2)}) collective-permute-start(f32[3,5,2048]{2,1,0:T(8,128)} %get-tuple-element.15), channel_id=1, source_target_pairs={{0,8},{8,16},{16,24},{24,0},{1,9},{9,17},{17,25},{25,1},{2,10},{10... | collective-permute-start | bytes 368648 | tf_op jit(solution)/shard_map/ppermute | solution.py:16
  36.2 20.5 %collective-permute-start.1 = (f32[3,5,2048]{2,1,0:T(8,128)S(1)}, f32[3,5,2048]{2,1,0:T(8,128)S(1)}, u32[]{:S(2)}, u32[]{:S(2)}) collective-permute-start(f32[3,5,2048]{2,1,0:T(8,128)S(1)} %get-tuple-element.16), channel_id=1, source_target_pairs={{8,0},{16,8},{24,16},{0,24},{9,1},{17,9},{25,17},{1,25},{10,2},{18... | collective-permute-start | bytes 368648 | tf_op jit(solution)/shard_map/ppermute | solution.py:19
  39.4 10.2 %collective-permute-start.6 = (f32[8,66,1]{2,1,0:T(8,128)S(1)}, f32[8,66,1]{2,1,0:T(8,128)S(1)}, u32[]{:S(2)}, u32[]{:S(2)}) collective-permute-start(f32[8,66,1]{2,1,0:T(8,128)S(1)} %get-tuple-element.5), channel_id=1, source_target_pairs={{2,0},{4,2},{6,4},{0,6},{3,1},{5,3},{7,5},{1,7},{10,8},{12,10},{14... | collective-permute-start | bytes 6344 | tf_op jit(solution)/shard_map/ppermute | solution.py:19
  40.9 8.8 %collective-permute-start.7 = (f32[8,66,1]{2,1,0:T(8,128)S(1)}, f32[8,66,1]{2,1,0:T(8,128)S(1)}, u32[]{:S(2)}, u32[]{:S(2)}) collective-permute-start(f32[8,66,1]{2,1,0:T(8,128)S(1)} %get-tuple-element.6), channel_id=1, source_target_pairs={{0,2},{2,4},{4,6},{6,0},{1,3},{3,5},{5,7},{7,1},{8,10},{10,12},{12... | collective-permute-start | bytes 6344 | tf_op jit(solution)/shard_map/ppermute | solution.py:16
  42.6 14.1 %copy-start.1 = (f32[2,64,2048]{2,1,0:T(8,128)S(1)}, f32[2,64,2048]{2,1,0:T(8,128)}, u32[]{:S(2)}) copy-start(f32[2,64,2048]{2,1,0:T(8,128)} %all-gather.2.cloned.1.call-done) | copy-start | bytes 3145732
  49.7 7.0 %copy-start.5 = (f32[8,66,1]{2,1,0:T(8,128)}, f32[8,66,1]{2,1,0:T(8,128)S(1)}, u32[]{:S(2)}) copy-start(f32[8,66,1]{2,1,0:T(8,128)S(1)} %collective-permute-done.6) | copy-start | bytes 6340
  49.7 7.0 %copy-start.6 = (f32[8,66,1]{2,1,0:T(8,128)}, f32[8,66,1]{2,1,0:T(8,128)S(1)}, u32[]{:S(2)}) copy-start(f32[8,66,1]{2,1,0:T(8,128)S(1)} %collective-permute-done.7) | copy-start | bytes 6340
  57.0 6.2 %copy-start.2 = (f32[3,74,2048]{2,1,0:T(8,128)}, f32[3,74,2048]{2,1,0:T(8,128)S(1)}, u32[]{:S(2)}) copy-start(f32[3,74,2048]{2,1,0:T(8,128)S(1)} %pad_maximum_fusion.11) | copy-start | bytes 5455876
  57.1 6.1 %collective-permute-start.3 = (f32[3,74,5]{2,1,0:T(8,128)S(1)}, f32[3,74,5]{2,1,0:T(8,128)S(1)}, u32[]{:S(2)}, u32[]{:S(2)}) collective-permute-start(f32[3,74,5]{2,1,0:T(8,128)S(1)} %get-tuple-element.13), channel_id=1, source_target_pairs={{2,0},{4,2},{6,4},{0,6},{3,1},{5,3},{7,5},{1,7},{10,8},{12,10},{14... | collective-permute-start | bytes 13328 | tf_op jit(solution)/shard_map/ppermute | solution.py:19
  57.6 6.2 %collective-permute-start.2 = (f32[3,74,5]{2,1,0:T(8,128)S(1)}, f32[3,74,5]{2,1,0:T(8,128)}, u32[]{:S(2)}, u32[]{:S(2)}) collective-permute-start(f32[3,74,5]{2,1,0:T(8,128)S(1)} %get-tuple-element.14), channel_id=1, source_target_pairs={{0,2},{2,4},{4,6},{6,0},{1,3},{3,5},{5,7},{7,1},{8,10},{10,12},{12... | collective-permute-start | bytes 13328 | tf_op jit(solution)/shard_map/ppermute | solution.py:16
  61.1 21.1 %collective-permute-start.8 = (f32[66,2050]{1,0:T(8,128)}, f32[66,2050]{1,0:T(8,128)}, u32[]{:S(2)}, u32[]{:S(2)}) collective-permute-start(f32[66,2050]{1,0:T(8,128)} %fusion.75), channel_id=1, source_target_pairs={{0,1},{1,0},{2,3},{3,2},{4,5},{5,4},{6,7},{7,6},{8,9},{9,8},{10,11... | collective-permute-start | bytes 1623608 | tf_op jit(solution)/shard_map/ppermute | solution.py:27
  63.2 0.6 copy-start.7
  75.6 1.4 %copy-start.4 = (f32[1,64,2048]{2,1,0:T(8,128)S(1)}, f32[1,64,2048]{2,1,0:T(8,128)}, u32[]{:S(2)}) copy-start(f32[1,64,2048]{2,1,0:T(8,128)} %copy-done.3) | copy-start | bytes 1572868
  75.6 1.4 %copy-start.8 = (f32[3,74,5]{2,1,0:T(8,128)S(1)}, f32[3,74,5]{2,1,0:T(8,128)}, u32[]{:S(2)}) copy-start(f32[3,74,5]{2,1,0:T(8,128)} %copy-done.7) | copy-start | bytes 13324
  76.3 5.9 %slice-start = ((s8[5013504]{0:T(1024)(128)(4,1)}), s8[4194304]{0:T(1024)(128)(4,1)S(1)}, s32[]{:S(2)}) async-start(s8[5013504]{0:T(1024)(128)(4,1)} %bitcast.72), calls=%async_computation.1 | async-start | bytes 8388608
  76.9 5.3 %slice-start.1 = ((s8[5013504]{0:T(1024)(128)(4,1)}), s8[819200]{0:T(1024)(128)(4,1)S(1)}, s32[]{:S(2)}) async-start(s8[5013504]{0:T(1024)(128)(4,1)} %bitcast.72), calls=%async_computation.2 | async-start | bytes 1638400
  80.2 4.1 %copy-start = (f32[8,64,2048]{2,1,0:T(8,128)S(1)}, f32[8,64,2048]{2,1,0:T(8,128)}, u32[]{:S(2)}) copy-start(f32[8,64,2048]{2,1,0:T(8,128)} %param.7) | copy-start | bytes 12582916
  80.2 4.1 %copy-start.10 = (f32[8,1,2048]{2,1,0:T(1,128)S(1)}, f32[8,1,2048]{2,1,0:T(1,128)}, u32[]{:S(2)}) copy-start(f32[8,1,2048]{2,1,0:T(1,128)} %copy-done.9) | copy-start | bytes 196612
Sparse Core Ops, SparseCore 0:
  10.1 23.1 all-gather.1
where the time goes:
time: 122 us; the launch traced here: 121 us
  other arithmetic  59.5 us (49%)
  waiting for transfers between devices  21 us (17%)
  local copies, waits for them, and re-layouts  14.5 us (12%)
  between operations  14.3 us (12%)
  starting transfers between devices  12.2 us (10%)
    add x1, other arithmetic, shards(): second_north + second_east + 2.0 * slope_north * mixed_north  30.3 us
    all_gather x1, waiting for transfers between devices, shards(): surface_tile = lax.all_gather(surface_pair, 'gz', axis=2, tiled=True)  11.1 us
    concatenate x2, local copies, waits for them, and re-layouts, with_halo(): block = jnp.concatenate([low, block, high], axis=dim)  9.94 us
    ppermute x4, waiting for transfers between devices, with_halo(): lax.ppermute(lax.slice_in_dim(block, 0, width, axis=dim), axis, backward)  9.24 us
    ppermute x4, starting transfers between devices, with_halo(): lax.ppermute(lax.slice_in_dim(block, 0, width, axis=dim), axis, backward)  6.1 us
    concatenate x2, other arithmetic, with_halo(): block = jnp.concatenate([low, block, high], axis=dim)  5.81 us
    ppermute x4, starting transfers between devices, with_halo(): lax.ppermute(lax.slice_in_dim(block, block.shape[dim] - width, None, axis...  5.81 us
    div x2, other arithmetic, rates(): (8.0 * (window(extended, 1, 0, 2) - window(extended, -1, 0, 2)) - (window...  4.83 us
  transfers between devices with their start and end apart: 10, of which 5 were waited for; matrix products, arithmetic and copies ran while one was open for 30% of the time, Pallas kernels for 0%

commit v1 on v0

v1 whole, which is shorter than its diff:
```python
import functools

import jax
import jax.numpy as jnp
from jax import lax
from jax.experimental import pallas as pl
from jax.experimental.pallas import tpu as pltpu
from jax.sharding import PartitionSpec as P

time_step = 0.05
depth_unit = 0.015625
LANES = 128
SUBS = 8


def shift_rows(prev, cur, nxt, step):
    sub = lax.broadcasted_iota(jnp.int32, cur.shape, 0)
    if step < 0:
        return pltpu.roll(jnp.where(sub >= SUBS + step, prev, cur), -step, 0)
    return pltpu.roll(jnp.where(sub < step, nxt, cur), SUBS - step, 0)


def shift_lanes(left, cur, right, step):
    lane = lax.broadcasted_iota(jnp.int32, cur.shape, 1)
    if step < 0:
        return pltpu.roll(jnp.where(lane >= LANES + step, left, cur), -step, 1)
    return pltpu.roll(jnp.where(lane < step, right, cur), LANES - step, 1)


def square(tile, at_end):
    rest = jnp.zeros((LANES - tile.shape[0], LANES), tile.dtype)
    return jnp.concatenate([rest, tile] if at_end else [tile, rest], 0)


def first_pack(group, e_left, e_right, p_left, p_right, layer, seam, outer, layer_out):
    left = jnp.concatenate([e_left[...], p_left[...]], 0).T[:SUBS]
    right = jnp.concatenate([e_right[...], p_right[...]], 0).T[LANES - SUBS :]
    low = group[0] == 0
    seam[...] = jnp.where(low, right, left)
    outer[...] = jnp.where(low, left, right)
    layer_out[...] = layer[0]


def lazy_pack(v_top, v_bottom, v_left, v_right, s_top, s_bottom, s_left, s_right, up, down, to_right, to_left):
    layers, _, width = v_top.shape
    piece = width // SUBS
    for k in range(layers):
        up[k : k + 1, :width] = v_bottom[k, SUBS - 1 : SUBS, :]
        down[k : k + 1, :width] = v_top[k, 0:1, :]
    for q in range(SUBS):
        part = slice(q * piece, (q + 1) * piece)
        up[q : q + 1, width:] = s_bottom[SUBS - 1 : SUBS, part].astype(jnp.float32) * depth_unit
        down[q : q + 1, width:] = s_top[0:1, part].astype(jnp.float32) * depth_unit
    to_right[...] = jnp.zeros_like(to_right)
    to_left[...] = jnp.zeros_like(to_left)
    for j in range(layers // 2):
        both = jnp.concatenate([v_right[2 * j], v_right[2 * j + 1]], 0).T
        to_right[j : j + 1, :] = both[LANES - 1 :]
        both = jnp.concatenate([v_left[2 * j], v_left[2 * j + 1]], 0).T
        to_left[j : j + 1, :] = both[:1]
    j = layers // 2
    both = jnp.concatenate([s_right[...], s_right[...]], 0).astype(jnp.float32) * depth_unit
    to_right[j : j + 1, :] = both.T[LANES - 1 :]
    both = jnp.concatenate([s_left[...], s_left[...]], 0).astype(jnp.float32) * depth_unit
    to_left[j : j + 1, :] = both.T[:1]


def side_blocks(low, seam, outer):
    left = square(jnp.where(low, outer, seam), True).T
    right = square(jnp.where(low, seam, outer), False).T
    return left, right


def row_pack(group, e_top, e_bottom, p_top, p_bottom, seam, outer, up, down):
    left, right = side_blocks(group[0] == 0, seam[...], outer[...])
    rows = LANES // 2
    width = e_top.shape[1]
    for row, tops, bottoms in ((0, e_top, e_bottom), (SUBS, p_top, p_bottom)):
        base = 0 if row == 0 else rows
        up[row : row + SUBS, :LANES] = left[base + rows - SUBS : base + rows]
        up[row : row + SUBS, LANES : LANES + width] = bottoms[...]
        up[row : row + SUBS, LANES + width :] = right[base + rows - SUBS : base + rows]
        down[row : row + SUBS, :LANES] = left[base : base + SUBS]
        down[row : row + SUBS, LANES : LANES + width] = tops[...]
        down[row : row + SUBS, LANES + width :] = right[base : base + SUBS]


def neighbourhood(ref, block, lane, blocks):
    here = pl.multiple_of(block * SUBS, SUBS)
    above = pl.multiple_of(jnp.maximum(block - 1, 0) * SUBS, SUBS)
    below = pl.multiple_of(jnp.minimum(block + 1, blocks - 1) * SUBS, SUBS)
    at = lambda row, column: ref[pl.ds(row, SUBS), column : column + LANES]
    cur = at(here, lane)
    prev, nxt = at(above, lane), at(below, lane)
    left, right = at(here, lane - LANES), at(here, lane + LANES)
    rows = [shift_rows(prev, cur, nxt, step) for step in (-2, -1, 1, 2)]
    lanes = [shift_lanes(left, cur, right, step) for step in (-2, -1, 1, 2)]
    return cur, rows, lanes


def slope(values):
    return (8.0 * (values[2] - values[1]) - (values[3] - values[0])) * (1.0 / 12.0)


def tile_rates(e_near, p_near):
    e, e_rows, e_lanes = e_near
    p, p_rows, p_lanes = p_near
    p_x, p_y = slope(p_rows), slope(p_lanes)
    bend = 16.0 * ((p_rows[1] + p_rows[2]) + (p_lanes[1] + p_lanes[2]))
    bend = bend - ((p_rows[0] + p_rows[3]) + (p_lanes[0] + p_lanes[3])) - 60.0 * p
    rate_e = bend * (1.0 / 12.0) - (slope(e_rows) * p_x + slope(e_lanes) * p_y)
    rate_p = -e - 0.5 * (p_x * p_x + p_y * p_y)
    return e, p, rate_e, rate_p


def surface(
    group, e, p, seam, outer, north, south, far_north, far_south, x_left, x_right,
    new_e, new_p, wide_e, wide_p, rims, e0, p0, e1, p1,
):
    rows, width = e.shape
    low = group[0] == 0
    left, right = side_blocks(low, seam[...], outer[...])
    blocks = rows // SUBS + 2
    pad = 2 * LANES
    for old, source, base in ((e0, e, 0), (p0, p, LANES // 2)):
        half = SUBS if base else 0
        old[:SUBS, LANES : LANES + width + pad] = north[half : half + SUBS, :]
        old[rows + SUBS :, LANES : LANES + width + pad] = south[half : half + SUBS, :]
        old[SUBS : SUBS + rows, pad : pad + width] = source[...]
        old[SUBS : SUBS + rows, LANES:pad] = left[base : base + rows]
        old[SUBS : SUBS + rows, pad + width : pad + width + LANES] = right[base : base + rows]
    chunks = range(LANES, width + 3 * LANES, LANES)

    def first(block, carry):
        here = pl.multiple_of(block * SUBS, SUBS)
        for lane in chunks:
            old_e, old_p, rate_e, rate_p = tile_rates(
                neighbourhood(e0, block, lane, blocks), neighbourhood(p0, block, lane, blocks)
            )
            e1[pl.ds(here, SUBS), lane : lane + LANES] = old_e + time_step * rate_e
            p1[pl.ds(here, SUBS), lane : lane + LANES] = old_p + time_step * rate_p
        return carry

    lax.fori_loop(0, blocks, first, 0)

    def second(block, carry):
        here = pl.multiple_of(block * SUBS, SUBS)
        for lane in chunks:
            one_e, one_p, rate_e, rate_p = tile_rates(
                neighbourhood(e1, block, lane, blocks), neighbourhood(p1, block, lane, blocks)
            )
            old_e = e0[pl.ds(here, SUBS), lane : lane + LANES]
            old_p = p0[pl.ds(here, SUBS), lane : lane + LANES]
            to = lane - LANES
            wide_e[pl.ds(here, SUBS), to : to + LANES] = 0.5 * (old_e + one_e + time_step * rate_e)
            wide_p[pl.ds(here, SUBS), to : to + LANES] = 0.5 * (old_p + one_p + time_step * rate_p)
        return carry

    lax.fori_loop(0, blocks, second, 0)
    new_e[...] = wide_e[SUBS : SUBS + rows, LANES : LANES + width]
    new_p[...] = wide_p[SUBS : SUBS + rows, LANES : LANES + width]
    rims[...] = jnp.zeros_like(rims)
    layers = far_north.shape[0]
    tile = 2 * width
    rims[0:1, :] = jnp.where(low, far_north[layers - 1 : layers, :tile], far_north[0:1, :tile])
    rims[1:2, :] = jnp.where(low, far_south[layers - 1 : layers, :tile], far_south[0:1, :tile])
    for row, wide in ((2, wide_e), (3, wide_p)):
        rims[row : row + 1, :width] = wide[SUBS - 1 : SUBS, LANES : LANES + width]
        rims[row : row + 1, width:] = wide[SUBS + rows : SUBS + rows + 1, LANES : LANES + width]
    pairs = layers // 2
    for lane, side in ((0, x_left), (LANES, x_right)):
        top_pair = pltpu.roll(side[...], LANES // 2, 1)[pairs - 1 : pairs]
        rims[4:5, lane : lane + LANES] = jnp.where(low, top_pair, side[0:1, :])
    inner = slice(SUBS, SUBS + rows)
    left = jnp.concatenate([wide_e[inner, :LANES], wide_p[inner, :LANES]], 0).T[LANES - 1 :]
    right = jnp.concatenate([wide_e[inner, LANES + width :], wide_p[inner, LANES + width :]], 0).T[:1]
    rims[4:5, 2 * LANES : 3 * LANES] = jnp.where(low, left, right)


def widen(low, group, wide, other, rims, row, base, target):
    rows, width = other.shape
    inner = slice(SUBS, SUBS + rows)
    own = pl.multiple_of(LANES + group * width, LANES)
    far = pl.multiple_of(LANES + (1 - group) * width, LANES)
    own_side = pl.multiple_of(group * (2 * width + LANES), LANES)
    far_side = pl.multiple_of((1 - group) * (2 * width + LANES), LANES)
    target[:, pl.ds(own, width)] = wide[:, LANES : LANES + width]
    target[:, pl.ds(own_side, LANES)] = jnp.where(low, wide[:, :LANES], wide[:, LANES + width :])
    target[inner, pl.ds(far, width)] = other[...]
    target[SUBS - 1 : SUBS, pl.ds(far, width)] = rims[row : row + 1, :width]
    target[SUBS + rows : SUBS + rows + 1, pl.ds(far, width)] = rims[row : row + 1, width:]
    column = square(rims[:, 2 * LANES : 3 * LANES], False).T[base : base + rows]
    column = jnp.where(low, pltpu.roll(column, LANES - 4, 1), pltpu.roll(column, LANES - 5, 1))
    target[inner, pl.ds(far_side, LANES)] = column


def laplace(
    total_layers, group_ref, v, far_layer, sea, far_north, far_south, x_left, x_right, rims, wide_e, other_e,
    out, coefficients, volume, column, depth, sems,
):
    block = pl.program_id(0)
    group = group_ref[0]
    low = group == 0
    layers, rows, tile = v.shape
    blocks = rows // SUBS
    inner = slice(SUBS, SUBS + rows)
    far_slot = jnp.where(low, layers + 1, 0)
    own_slot = layers + 1 - far_slot
    own_source = jnp.where(low, 0, layers - 1)

    def copies(index):
        part = pl.ds(pl.multiple_of(index * SUBS, SUBS), SUBS)
        into = pl.ds(pl.multiple_of((index + 1) * SUBS, SUBS), SUBS)
        return (
            pltpu.make_async_copy(
                v.at[:, part, :], volume.at[1 : layers + 1, into, LANES : LANES + tile], sems.at[0, index]
            ),
            pltpu.make_async_copy(
                v.at[own_source, part, :], volume.at[own_slot, into, LANES : LANES + tile], sems.at[1, index]
            ),
            pltpu.make_async_copy(
                far_layer.at[part, :], volume.at[far_slot, into, LANES : LANES + tile], sems.at[2, index]
            ),
        )

    @pl.when(block == 0)
    def _():
        for index in range(blocks):
            for copy in copies(index):
                copy.start()
        left = square(x_left[...], False).T
        right = square(x_right[...], False).T
        half = LANES // 2
        pairs = layers // 2

        def sides(slot, from_left, from_right, north, south):
            volume[slot, inner, :LANES] = from_left
            volume[slot, inner, LANES + tile :] = from_right
            volume[slot, SUBS - 1 : SUBS, LANES : LANES + tile] = north
            volume[slot, SUBS + rows : SUBS + rows + 1, LANES : LANES + tile] = south

        def own_sides(k):
            base = (k % 2) * half
            return (
                pltpu.roll(left, LANES - 1 - k // 2, 1)[base : base + rows],
                pltpu.roll(right, (LANES - k // 2) % LANES, 1)[base : base + rows],
                far_north[k : k + 1, :tile],
                far_south[k : k + 1, :tile],
            )

        for k in range(layers):
            sides(k + 1, *own_sides(k))
        first, last = own_sides(0), own_sides(layers - 1)
        sides(own_slot, *(jnp.where(low, a, b) for a, b in zip(first, last)))
        far_left = pltpu.roll(square(rims[:, :LANES], False).T, LANES - 5, 1)[:rows]
        far_right = pltpu.roll(square(rims[:, LANES : 2 * LANES], False).T, LANES - 4, 1)[:rows]
        sides(far_slot, far_left, far_right, rims[0:1, :], rims[1:2, :])

        depth[inner, LANES : LANES + tile] = sea[...].astype(jnp.float32) * depth_unit
        piece = tile // SUBS
        for q in range(SUBS):
            part = slice(LANES + q * piece, LANES + (q + 1) * piece)
            depth[SUBS - 1 : SUBS, part] = far_north[q : q + 1, tile:]
            depth[SUBS + rows : SUBS + rows + 1, part] = far_south[q : q + 1, tile:]
        depth[inner, :LANES] = pltpu.roll(left, LANES - 1 - pairs, 1)[:rows]
        depth[inner, LANES + tile :] = pltpu.roll(right, LANES - pairs, 1)[:rows]
        widen(low, group, wide_e, other_e, rims, 2, 0, column)
        column[...] = column[...] + depth[...]
        for copy in copies(0):
            copy.wait()

    @pl.when(block < blocks - 1)
    def _():
        for copy in copies(block + 1):
            copy.wait()

    spacing = 1.0 / total_layers
    sigma = (group * layers).astype(jnp.float32) * spacing + 0.5 * spacing
    sign = (1 - 2 * group).astype(jnp.float32)
    here = pl.multiple_of((block + 1) * SUBS, SUBS)
    above = pl.multiple_of(block * SUBS, SUBS)
    below = pl.multiple_of((block + 2) * SUBS, SUBS)

    def near(ref, lane):
        at = lambda row, start: ref[pl.ds(row, SUBS), pl.ds(start, LANES)]
        cur = at(here, lane)
        prev, nxt = at(above, lane), at(below, lane)
        left = at(here, pl.multiple_of(lane - LANES, LANES))
        right = at(here, pl.multiple_of(lane + LANES, LANES))
        return (
            cur,
            shift_rows(prev, cur, nxt, -1),
            shift_rows(prev, cur, nxt, 1),
            shift_lanes(left, cur, right, -1),
            shift_lanes(left, cur, right, 1),
        )

    def chunk(lane):
        to = pl.multiple_of(lane - LANES, LANES)
        c, c_up, c_down, c_left, c_right = near(column, lane)
        _, d_up, d_down, d_left, d_right = near(depth, lane)
        inverse = 1.0 / c
        scale = (0.25 / spacing) * inverse
        bx, by = scale * (c_down - c_up), scale * (c_right - c_left)
        ax, ay = scale * (d_down - d_up), scale * (d_right - d_left)
        ux, uy = ax - sigma * bx, ay - sigma * by
        bx, by = spacing * bx, spacing * by
        scaled = inverse * (1.0 / spacing)
        weight = 4.0 * (ux * ux + uy * uy) + scaled * scaled
        bend = 4.0 * (bx * bx + by * by)
        step = bend - 8.0 * (ux * bx + uy * by)
        bend = bend + bend

        def level(slot):
            p, up, down, left, right = near(volume.at[slot], lane)
            return p, down - up, right - left, (down + up) + (right + left)

        below_level = level(0)
        this = level(1)
        for k in range(layers):
            above_level = level(k + 2)
            p, north, east, _ = above_level
            if k == layers - 1:
                p, north, east = sign * p, sign * north, sign * east
            centre = this[0]
            twice = centre + centre
            value = this[3] - (twice + twice)
            value = value + ux * (north - below_level[1]) + uy * (east - below_level[2])
            value = value + weight * ((p + below_level[0]) - twice)
            out[k, :, pl.ds(to, LANES)] = value
            if k == layers - 1:
                coefficients[0, :, pl.ds(to, LANES)] = ux
                coefficients[1, :, pl.ds(to, LANES)] = uy
                coefficients[2, :, pl.ds(to, LANES)] = weight
            else:
                ux, uy = ux - bx, uy - by
                weight, step = weight + step, step + bend
            below_level, this = this, above_level

    group_of = 2

    def pair(index, carry):
        for inside in range(group_of):
            chunk(pl.multiple_of((index * group_of + inside + 1) * LANES, LANES))
        return carry

    lax.fori_loop(0, tile // LANES // group_of, pair, 0)


def top(group_ref, before, coefficients, rims, wide_p, other_p, out, potential):
    group = group_ref[0]
    low = group == 0
    rows, tile = before.shape[1], before.shape[2]
    widen(low, group, wide_p, other_p, rims, 3, LANES // 2, potential)
    gain = 2.0 * group.astype(jnp.float32)

    def body(block, carry):
        here = pl.multiple_of((block + 1) * SUBS, SUBS)
        above = pl.multiple_of(block * SUBS, SUBS)
        below = pl.multiple_of((block + 2) * SUBS, SUBS)
        for lane in range(LANES, LANES + tile, LANES):
            at = lambda row, start: potential[pl.ds(row, SUBS), start : start + LANES]
            cur = at(here, lane)
            prev, nxt = at(above, lane), at(below, lane)
            left, right = at(here, lane - LANES), at(here, lane + LANES)
            north = shift_rows(prev, cur, nxt, 1) - shift_rows(prev, cur, nxt, -1)
            east = shift_lanes(left, cur, right, 1) - shift_lanes(left, cur, right, -1)
            spot = (pl.ds(above, SUBS), slice(lane - LANES, lane))
            value = coefficients[(0, *spot)] * north + coefficients[(1, *spot)] * east
            value = value + coefficients[(2, *spot)] * cur
            out[(0, *spot)] = before[(0, *spot)] + gain * value
        return carry

    lax.fori_loop(0, rows // SUBS, body, 0)


def ring(axis, step):
    count = lax.axis_size(axis)
    return [(i, (i + step) % count) for i in range(count)]


def shards(elevation, surface_potential, seabed, interior_potential):
    rows, width = elevation.shape
    layers, _, tile = interior_potential.shape
    assert 2 * rows == LANES and tile == 2 * width and layers == SUBS
    assert lax.axis_size("gz") == 2
    total_layers = layers * lax.axis_size("gz")
    f32 = jnp.float32
    shape = lambda *dims: jax.ShapeDtypeStruct(dims, f32)
    whole = lambda *dims: pl.BlockSpec(dims, lambda *_: (0,) * len(dims))
    group = lax.axis_index("gz").astype(jnp.int32).reshape((1,))
    scalar = pl.BlockSpec(memory_space=pltpu.SMEM)
    last_row, last_half, last_tile = rows // SUBS - 1, width // LANES - 1, tile // LANES - 1

    def block(dims, *index):
        return pl.BlockSpec(dims, lambda *_: index)

    params = pltpu.CompilerParams(vmem_limit_bytes=40 * 1024 * 1024)
    seam, outer, layer = pl.pallas_call(
        first_pack,
        out_shape=(shape(SUBS, LANES), shape(SUBS, LANES), shape(rows, tile)),
        grid_spec=pltpu.PrefetchScalarGridSpec(
            num_scalar_prefetch=1,
            grid=(1,),
            in_specs=[
                block((rows, LANES), 0, 0),
                block((rows, LANES), 0, last_half),
                block((rows, LANES), 0, 0),
                block((rows, LANES), 0, last_half),
                pl.BlockSpec((1, rows, tile), lambda _, g: (jnp.where(g[0] == 0, layers - 1, 0), 0, 0)),
            ],
            out_specs=[whole(SUBS, LANES), whole(SUBS, LANES), whole(rows, tile)],
        ),
        compiler_params=params,
        name="first_pack",
    )(group, elevation, elevation, surface_potential, surface_potential, interior_potential)

    flat = ("gy", "gz")
    count = lax.axis_size("gy")
    partner = [(2 * i + g, 2 * i + 1 - g) for i in range(count) for g in range(2)]
    across = [(2 * i + 1, (2 * i + 2) % (2 * count)) for i in range(count)]
    across = across + [(b, a) for a, b in across]
    with jax.named_scope("seam"):
        seam = lax.ppermute(seam, flat, partner)
    with jax.named_scope("outer"):
        outer = lax.ppermute(outer, flat, across)
    with jax.named_scope("layer"):
        far_layer = lax.ppermute(layer, flat, partner)

    up, down, to_right, to_left = pl.pallas_call(
        lazy_pack,
        out_shape=(shape(SUBS, tile + tile // SUBS),) * 2 + (shape(SUBS, LANES),) * 2,
        grid=(1,),
        in_specs=[
            block((layers, SUBS, tile), 0, 0, 0),
            block((layers, SUBS, tile), 0, last_row, 0),
            block((layers, rows, LANES), 0, 0, 0),
            block((layers, rows, LANES), 0, 0, last_tile),
            block((SUBS, tile), 0, 0),
            block((SUBS, tile), last_row, 0),
            block((rows, LANES), 0, 0),
            block((rows, LANES), 0, last_tile),
        ],
        out_specs=[whole(SUBS, tile + tile // SUBS)] * 2 + [whole(SUBS, LANES)] * 2,
        compiler_params=params,
        name="lazy_pack",
    )(*(interior_potential,) * 4, *(seabed,) * 4)

    wide = width + 2 * LANES
    row_up, row_down = pl.pallas_call(
        row_pack,
        out_shape=(shape(2 * SUBS, wide),) * 2,
        grid=(1,),
        in_specs=[
            scalar,
            block((SUBS, width), 0, 0),
            block((SUBS, width), last_row, 0),
            block((SUBS, width), 0, 0),
            block((SUBS, width), last_row, 0),
            whole(SUBS, LANES),
            whole(SUBS, LANES),
        ],
        out_specs=[whole(2 * SUBS, wide)] * 2,
        compiler_params=params,
        name="row_pack",
    )(group, elevation, elevation, surface_potential, surface_potential, seam, outer)
    with jax.named_scope("rows"):
        north = lax.ppermute(row_up, "gx", ring("gx", 1))
        south = lax.ppermute(row_down, "gx", ring("gx", -1))
    with jax.named_scope("far"):
        far_north = lax.ppermute(up, "gx", ring("gx", 1))
        far_south = lax.ppermute(down, "gx", ring("gx", -1))
        x_left = lax.ppermute(to_right, "gy", ring("gy", 1))
        x_right = lax.ppermute(to_left, "gy", ring("gy", -1))

    deep = rows + 2 * SUBS
    scratch = pltpu.VMEM((deep, wide + 2 * LANES), f32)
    new_e, new_p, wide_e, wide_p, rims = pl.pallas_call(
        surface,
        out_shape=(shape(rows, width),) * 2 + (shape(deep, wide),) * 2 + (shape(SUBS, tile),),
        in_specs=[scalar] + [pl.BlockSpec(memory_space=pltpu.VMEM)] * 10,
        out_specs=[pl.BlockSpec(memory_space=pltpu.VMEM)] * 5,
        scratch_shapes=[scratch] * 4,
        compiler_params=params,
        name="surface",
    )(
        group, elevation, surface_potential, seam, outer, north, south,
        far_north, far_south, x_left, x_right,
    )
    with jax.named_scope("rims"):
        far_rims = lax.ppermute(rims, flat, partner)
    with jax.named_scope("height"):
        other_e = lax.ppermute(new_e, flat, partner)
    with jax.named_scope("potential"):
        other_p = lax.ppermute(new_p, flat, partner)

    blocks = rows // SUBS
    anywhere = pl.BlockSpec(memory_space=pl.ANY)
    partial, coefficients = pl.pallas_call(
        functools.partial(laplace, total_layers),
        out_shape=(shape(layers, rows, tile), shape(3, rows, tile)),
        grid=(blocks,),
        in_specs=[
            scalar,
            anywhere,
            anywhere,
            whole(rows, tile),
            whole(SUBS, tile + tile // SUBS),
            whole(SUBS, tile + tile // SUBS),
            whole(SUBS, LANES),
            whole(SUBS, LANES),
            whole(SUBS, tile),
            whole(deep, wide),
            whole(rows, width),
        ],
        out_specs=[
            pl.BlockSpec((layers, SUBS, tile), lambda i: (0, i, 0)),
            pl.BlockSpec((3, SUBS, tile), lambda i: (0, i, 0)),
        ],
        scratch_shapes=[
            pltpu.VMEM((layers + 2, deep, tile + 2 * LANES), f32),
            pltpu.VMEM((deep, tile + 2 * LANES), f32),
            pltpu.VMEM((deep, tile + 2 * LANES), f32),
            pltpu.SemaphoreType.DMA((3, blocks)),
        ],
        compiler_params=params,
        name="laplace",
    )(
        group, interior_potential, far_layer, seabed, far_north, far_south,
        x_left, x_right, far_rims, wide_e, other_e,
    )
    last_layer = pl.BlockSpec((1, rows, tile), lambda i: (layers - 1, 0, 0))
    result = pl.pallas_call(
        top,
        out_shape=shape(layers, rows, tile),
        grid=(1,),
        in_specs=[
            scalar,
            last_layer,
            whole(3, rows, tile),
            whole(SUBS, tile),
            whole(deep, wide),
            whole(rows, width),
        ],
        out_specs=last_layer,
        scratch_shapes=[pltpu.VMEM((deep, tile + 2 * LANES), f32)],
        input_output_aliases={1: 0},
        compiler_params=params,
        name="top",
    )(group, partial, coefficients, far_rims, wide_p, other_p)
    return new_e, new_p, result


def solution(mesh):
    return jax.shard_map(
        shards,
        mesh=mesh,
        in_specs=(P("gx", ("gy", "gz")), P("gx", ("gy", "gz")), P("gx", "gy"), P("gz", "gx", "gy")),
        out_specs=(P("gx", ("gy", "gz")), P("gx", ("gy", "gz")), P("gz", "gx", "gy")),
        check_vma=False,
    )
```

time: 122 us -> 70.2 us (0.58)
  other arithmetic: 59.5 us -> 0 us
  Pallas kernels: 0 us -> 20.9 us
  between operations: 14.3 us -> 0.69 us
  local copies, waits for them, and re-layouts: 14.5 us -> 4.09 us
  waiting for transfers between devices: 21 us -> 28.3 us
  starting transfers between devices: 12.2 us -> 14.9 us
    add x3 -> x0, other arithmetic: 30.9 us -> none  [the longest x1 30.3 us: shards(): second_north + second_east + 2.0 * slope_north * mixed_north]
    pallas_call x0 -> x6, Pallas kernels: none -> 20.9 us  [the longest x1 13.4 us: shards(): pl.pallas_call(functools.partial(laplace, total_layers), out_shape=(shape...]
    ppermute x9 -> x12, waiting for transfers between devices: 9.84 us -> 28.3 us  [the longest x1 11.9 us: shards(): far_rims = lax.ppermute(rims, flat, partner)]
    all_gather x1 -> x0, waiting for transfers between devices: 11.1 us -> none  [shards(): surface_tile = lax.all_gather(surface_pair, 'gz', axis=2, tiled=True)]
    concatenate x2 -> x0, local copies, waits for them, and re-layouts: 9.94 us -> none  [with_halo(): block = jnp.concatenate([low, block, high], axis=dim)]
    concatenate x2 -> x0, other arithmetic: 5.81 us -> none  [with_halo(): block = jnp.concatenate([low, block, high], axis=dim)]
    div x3 -> x0, other arithmetic: 5.38 us -> none  [the longest x2 4.83 us: rates(): (8.0 * (window(extended, 1, 0, 2) - window(extended, -1, 0, 2)) - (window...]
    another operation x3 -> x0, other arithmetic: 4.67 us -> none  [the longest x2 2.8 us: rates(): return jnp.stack([rate_height, rate_potential])]
  transfers between devices with their start and end apart: 10 -> 12, of which waited for: 5 -> 7; matrix products, arithmetic and copies ran while one was open for 30% -> 0% of each run, Pallas kernels for 0% -> 26%
where the time goes in v1:
time: 70.2 us; the launch traced here: 68.9 us
  waiting for transfers between devices  28.3 us (40%)
  Pallas kernels  20.9 us (30%)
  starting transfers between devices  14.9 us (21%)
  local copies, waits for them, and re-layouts  4.09 us (6%)
    pallas_call x1, Pallas kernels, shards(): pl.pallas_call(functools.partial(laplace, total_layers), out_shape=(shape...  13.4 us
    ppermute x1, waiting for transfers between devices, shards(): far_rims = lax.ppermute(rims, flat, partner)  11.9 us
    ppermute x1, waiting for transfers between devices, shards(): seam = lax.ppermute(seam, flat, partner)  9.17 us
    pallas_call x1, Pallas kernels, shards(): pl.pallas_call(surface, out_shape=(shape(rows, width),) * 2 + (shape(deep...  4.2 us
    unnamed x10, local copies, waits for them, and re-layouts  4.09 us
    pallas_call x1, Pallas kernels, shards(): pl.pallas_call(top, out_shape=shape(layers, rows, tile), grid=(1,), in_sp...  3 us
    ppermute x1, starting transfers between devices, shards(): outer = lax.ppermute(outer, flat, across)  2.51 us
    ppermute x1, waiting for transfers between devices, shards(): x_right = lax.ppermute(to_left, 'gy', ring('gy', -1))  2.27 us
  transfers between devices with their start and end apart: 12, of which 7 were waited for; matrix products, arithmetic and copies ran while one was open for 0% of the time, Pallas kernels for 26%

profile of v1, /device:TPU:1, one launch (start us, length us, event | category | flops | bytes accessed | tf_op | source)
XLA Modules:
  0.0 68.9 jit_solution(15760732233889536433)
XLA Ops:
  0.6 2.2 %copy-done = f32[8,64,2048]{2,1,0:T(8,128)S(1)} copy-done((f32[8,64,2048]{2,1,0:T(8,128)S(1)}, f32[8,64,2048]{2,1,0:T(8,128)}, u32[]{:S(2)}) %copy-start) | copy-done | bytes 4194328
  2.8 0.9 %copy-done.3 = f32[64,1024]{1,0:T(8,128)S(1)} copy-done((f32[64,1024]{1,0:T(8,128)S(1)}, f32[64,1024]{1,0:T(8,128)}, u32[]{:S(2)}) %copy-start.3) | copy-done | bytes 262168
  3.8 0.9 %copy-done.4 = f32[64,1024]{1,0:T(8,128)S(1)} copy-done((f32[64,1024]{1,0:T(8,128)S(1)}, f32[64,1024]{1,0:T(8,128)}, u32[]{:S(2)}) %copy-start.4) | copy-done | bytes 262168
  4.8 2.1 %collective-permute-start.8 = (f32[64,2048]{1,0:T(8,128)S(1)}, f32[64,2048]{1,0:T(8,128)S(1)}, u32[]{:S(2)}, u32[]{:S(2)}) collective-permute-start(f32[64,2048]{1,0:T(8,128)S(1)} %get-tuple-element.29), channel_id=1, source_target_pairs={{0,1},{1,0},{2,3},{3,2},{4,5},{5,4},{6,7},{7,6},{8,9},{9,8},{10,11... | collective-permute-start | bytes 1572872 | tf_op jit(solution)/shard_map/layer/ppermute | solution.py:428
  6.9 0.1 collective-permute-start
  7.0 2.5 %collective-permute-start.1 = (f32[8,128]{1,0:T(8,128)S(1)}, f32[8,128]{1,0:T(8,128)S(1)}, u32[]{:S(2)}, u32[]{:S(2)}) collective-permute-start(f32[8,128]{1,0:T(8,128)S(1)} %get-tuple-element.20), channel_id=1, source_target_pairs={{1,2},{3,4},{5,6},{7,0},{2,1},{4,3},{6,5},{0,7},{9,10},{11,12},{13... | collective-permute-start | bytes 12296 | tf_op jit(solution)/shard_map/outer/ppermute | solution.py:426
  9.5 9.2 %collective-permute-done.seam = f32[8,128]{1,0:T(8,128)S(1)} collective-permute-done((f32[8,128]{1,0:T(8,128)S(1)}, f32[8,128]{1,0:T(8,128)S(1)}, u32[]{:S(2)}, u32[]{:S(2)}) %collective-permute-start) | collective-permute-done | bytes 4128 | tf_op jit(solution)/shard_map/seam/ppermute | solution.py:424
  18.7 0.9 %collective-permute-done.1.outer = f32[8,128]{1,0:T(8,128)S(1)} collective-permute-done((f32[8,128]{1,0:T(8,128)S(1)}, f32[8,128]{1,0:T(8,128)S(1)}, u32[]{:S(2)}, u32[]{:S(2)}) %collective-permute-start.1) | collective-permute-done | bytes 4128 | tf_op jit(solution)/shard_map/outer/ppermute | solution.py:426
  19.5 0.1 row_pack.1
  19.6 1.6 %collective-permute-start.2 = (f32[16,1280]{1,0:T(8,128)S(1)}, f32[16,1280]{1,0:T(8,128)S(1)}, u32[]{:S(2)}, u32[]{:S(2)}) collective-permute-start(f32[16,1280]{1,0:T(8,128)S(1)} %get-tuple-element.21), channel_id=1, source_target_pairs={{0,8},{8,16},{16,24},{24,0},{1,9},{9,17},{17,25},{25,1},{2,10},{10... | collective-permute-start | bytes 245768 | tf_op jit(solution)/shard_map/rows/ppermute | solution.py:468
  21.2 2.1 %collective-permute-start.3 = (f32[16,1280]{1,0:T(8,128)S(1)}, f32[16,1280]{1,0:T(8,128)S(1)}, u32[]{:S(2)}, u32[]{:S(2)}) collective-permute-start(f32[16,1280]{1,0:T(8,128)S(1)} %get-tuple-element.22), channel_id=1, source_target_pairs={{0,24},{8,0},{16,8},{24,16},{1,25},{9,1},{17,9},{25,17},{2,26},{10... | collective-permute-start | bytes 245768 | tf_op jit(solution)/shard_map/rows/ppermute | solution.py:469
  23.3 0.2 lazy_pack.1
  23.5 2.0 %collective-permute-start.6 = (f32[8,128]{1,0:T(8,128)S(1)}, f32[8,128]{1,0:T(8,128)S(1)}, u32[]{:S(2)}, u32[]{:S(2)}) collective-permute-start(f32[8,128]{1,0:T(8,128)S(1)} %get-tuple-element.25), channel_id=1, source_target_pairs={{0,2},{2,4},{4,6},{6,0},{1,3},{3,5},{5,7},{7,1},{8,10},{10,12},{12... | collective-permute-start | bytes 12296 | tf_op jit(solution)/shard_map/far/ppermute | solution.py:473
  25.5 0.8 %collective-permute-done.6.x_left = f32[8,128]{1,0:T(8,128)S(1)} collective-permute-done((f32[8,128]{1,0:T(8,128)S(1)}, f32[8,128]{1,0:T(8,128)S(1)}, u32[]{:S(2)}, u32[]{:S(2)}) %collective-permute-start.6) | collective-permute-done | bytes 4128 | tf_op jit(solution)/shard_map/far/ppermute | solution.py:473
  26.3 2.3 %collective-permute-done.7.x_right = f32[8,128]{1,0:T(8,128)S(1)} collective-permute-done((f32[8,128]{1,0:T(8,128)S(1)}, f32[8,128]{1,0:T(8,128)S(1)}, u32[]{:S(2)}, u32[]{:S(2)}) %collective-permute-start.7) | collective-permute-done | bytes 4128 | tf_op jit(solution)/shard_map/far/ppermute | solution.py:474
  28.6 1.5 %collective-permute-start.5 = (f32[8,2304]{1,0:T(8,128)S(1)}, f32[8,2304]{1,0:T(8,128)S(1)}, u32[]{:S(2)}, u32[]{:S(2)}) collective-permute-start(f32[8,2304]{1,0:T(8,128)S(1)} %get-tuple-element.24), channel_id=1, source_target_pairs={{0,24},{8,0},{16,8},{24,16},{1,25},{9,1},{17,9},{25,17},{2,26},{10... | collective-permute-start | bytes 221192 | tf_op jit(solution)/shard_map/far/ppermute | solution.py:472
  30.1 1.3 %collective-permute-done.4.far_north = f32[8,2304]{1,0:T(8,128)S(1)} collective-permute-done((f32[8,2304]{1,0:T(8,128)S(1)}, f32[8,2304]{1,0:T(8,128)S(1)}, u32[]{:S(2)}, u32[]{:S(2)}) %collective-permute-start.4) | collective-permute-done | bytes 73760 | tf_op jit(solution)/shard_map/far/ppermute | solution.py:471
  31.4 2.0 %collective-permute-done.5.far_south = f32[8,2304]{1,0:T(8,128)S(1)} collective-permute-done((f32[8,2304]{1,0:T(8,128)S(1)}, f32[8,2304]{1,0:T(8,128)S(1)}, u32[]{:S(2)}, u32[]{:S(2)}) %collective-permute-start.5) | collective-permute-done | bytes 73760 | tf_op jit(solution)/shard_map/far/ppermute | solution.py:472
  33.4 4.2 %surface.1 = (f32[64,1024]{1,0:T(8,128)}, f32[64,1024]{1,0:T(8,128)}, f32[80,1280]{1,0:T(8,128)S(1)}, f32[80,1280]{1,0:T(8,128)S(1)}, f32[8,2048]{1,0:T(8,128)S(1)}) custom-call(s32[1]{0:T(128)} %bitcast.group.group_ref, f32[64,1024]{1,0:T(8,128)S(1)} %copy-done.3, f32[64,1024]{1,0:T(8,128)S(1)} %copy-done.4, f32[8,128]{1,0:T(8,128)S(1)} %collective-permute-done.seam, ...), custom_call_target="tpu_custom_call" | custom-call | tf_op jit(solution)/shard_map/surface/pallas_call | solution.py:478
  37.6 1.5 %collective-permute-start.10 = (f32[64,1024]{1,0:T(8,128)}, f32[64,1024]{1,0:T(8,128)S(1)}, u32[]{:S(2)}, u32[]{:S(2)}) collective-permute-start(f32[64,1024]{1,0:T(8,128)} %get-tuple-element.16), channel_id=1, source_target_pairs={{0,1},{1,0},{2,3},{3,2},{4,5},{5,4},{6,7},{7,6},{8,9},{9,8},{10,11... | collective-permute-start | bytes 786440 | tf_op jit(solution)/shard_map/height/ppermute | solution.py:493
  39.1 1.4 %collective-permute-start.9 = (f32[8,2048]{1,0:T(8,128)S(1)}, f32[8,2048]{1,0:T(8,128)S(1)}, u32[]{:S(2)}, u32[]{:S(2)}) collective-permute-start(f32[8,2048]{1,0:T(8,128)S(1)} %get-tuple-element.30), channel_id=1, source_target_pairs={{0,1},{1,0},{2,3},{3,2},{4,5},{5,4},{6,7},{7,6},{8,9},{9,8},{10,11... | collective-permute-start | bytes 196616 | tf_op jit(solution)/shard_map/rims/ppermute | solution.py:491
  40.6 11.9 %collective-permute-done.9.rims = f32[8,2048]{1,0:T(8,128)S(1)} collective-permute-done((f32[8,2048]{1,0:T(8,128)S(1)}, f32[8,2048]{1,0:T(8,128)S(1)}, u32[]{:S(2)}, u32[]{:S(2)}) %collective-permute-start.9) | collective-permute-done | bytes 65568 | tf_op jit(solution)/shard_map/rims/ppermute | solution.py:491
  52.5 13.4 %laplace.1 = (f32[8,64,2048]{2,1,0:T(8,128)}, f32[3,64,2048]{2,1,0:T(8,128)S(1)}) custom-call(s32[1]{0:T(128)} %bitcast.group.group_ref, f32[8,64,2048]{2,1,0:T(8,128)S(1)} %copy-done.1, f32[64,2048]{1,0:T(8,128)S(1)} %collective-permute-done.8.far_layer, s32[64,2048]{1,0:T(8,128)S(1)} %copy-done.2, f32[8,2304]{1,0:T(8,128)S(1)} %collective-permute-done.4.far_north, ...), custom_call_target="tpu_custom_call" | custom-call | tf_op jit(solution)/shard_map/laplace/pallas_call | solution.py:499
  65.8 3.0 %top.1 = f32[8,64,2048]{2,1,0:T(8,128)} custom-call(s32[1]{0:T(128)} %bitcast.group.group_ref, f32[8,64,2048]{2,1,0:T(8,128)} %get-tuple-element.32.before, f32[3,64,2048]{2,1,0:T(8,128)S(1)} %get-tuple-element.33.coefficients, f32[8,2048]{1,0:T(8,128)S(1)} %collective-permute-done.9.rims, ...), custom_call_target="tpu_custom_call", output_to_operand_aliasing={{}: (1, {})} | custom-call | tf_op jit(solution)/shard_map/top/pallas_call | solution.py:533
  (16 shorter events, 0.1 us)
Async XLA Ops:
  0.6 2.2 %copy-start = (f32[8,64,2048]{2,1,0:T(8,128)S(1)}, f32[8,64,2048]{2,1,0:T(8,128)}, u32[]{:S(2)}) copy-start(f32[8,64,2048]{2,1,0:T(8,128)} %v.1) | copy-start | bytes 12582916
  2.8 0.9 %copy-start.3 = (f32[64,1024]{1,0:T(8,128)S(1)}, f32[64,1024]{1,0:T(8,128)}, u32[]{:S(2)}) copy-start(f32[64,1024]{1,0:T(8,128)} %e.1) | copy-start | bytes 786436
  3.8 0.9 %copy-start.4 = (f32[64,1024]{1,0:T(8,128)S(1)}, f32[64,1024]{1,0:T(8,128)}, u32[]{:S(2)}) copy-start(f32[64,1024]{1,0:T(8,128)} %p.1) | copy-start | bytes 786436
  4.7 18.6 %copy-start.1 = (f32[8,64,2048]{2,1,0:T(8,128)S(1)}, f32[8,64,2048]{2,1,0:T(8,128)}, u32[]{:S(2)}) copy-start(f32[8,64,2048]{2,1,0:T(8,128)} %v.1) | copy-start | bytes 12582916
  4.7 18.6 %copy-start.2 = (s32[64,2048]{1,0:T(8,128)S(1)}, s32[64,2048]{1,0:T(8,128)}, u32[]{:S(2)}) copy-start(s32[64,2048]{1,0:T(8,128)} %sea.1) | copy-start | bytes 1572868
  4.8 47.7 %collective-permute-start.8 = (f32[64,2048]{1,0:T(8,128)S(1)}, f32[64,2048]{1,0:T(8,128)S(1)}, u32[]{:S(2)}, u32[]{:S(2)}) collective-permute-start(f32[64,2048]{1,0:T(8,128)S(1)} %get-tuple-element.29), channel_id=1, source_target_pairs={{0,1},{1,0},{2,3},{3,2},{4,5},{5,4},{6,7},{7,6},{8,9},{9,8},{10,11... | collective-permute-start | bytes 1572872 | tf_op jit(solution)/shard_map/layer/ppermute | solution.py:428
  6.9 11.8 %collective-permute-start = (f32[8,128]{1,0:T(8,128)S(1)}, f32[8,128]{1,0:T(8,128)S(1)}, u32[]{:S(2)}, u32[]{:S(2)}) collective-permute-start(f32[8,128]{1,0:T(8,128)S(1)} %get-tuple-element.19), channel_id=1, source_target_pairs={{0,1},{1,0},{2,3},{3,2},{4,5},{5,4},{6,7},{7,6},{8,9},{9,8},{10,11... | collective-permute-start | bytes 12296 | tf_op jit(solution)/shard_map/seam/ppermute | solution.py:424
  7.0 12.5 %collective-permute-start.1 = (f32[8,128]{1,0:T(8,128)S(1)}, f32[8,128]{1,0:T(8,128)S(1)}, u32[]{:S(2)}, u32[]{:S(2)}) collective-permute-start(f32[8,128]{1,0:T(8,128)S(1)} %get-tuple-element.20), channel_id=1, source_target_pairs={{1,2},{3,4},{5,6},{7,0},{2,1},{4,3},{6,5},{0,7},{9,10},{11,12},{13... | collective-permute-start | bytes 12296 | tf_op jit(solution)/shard_map/outer/ppermute | solution.py:426
  19.6 13.7 %collective-permute-start.2 = (f32[16,1280]{1,0:T(8,128)S(1)}, f32[16,1280]{1,0:T(8,128)S(1)}, u32[]{:S(2)}, u32[]{:S(2)}) collective-permute-start(f32[16,1280]{1,0:T(8,128)S(1)} %get-tuple-element.21), channel_id=1, source_target_pairs={{0,8},{8,16},{16,24},{24,0},{1,9},{9,17},{17,25},{25,1},{2,10},{10... | collective-permute-start | bytes 245768 | tf_op jit(solution)/shard_map/rows/ppermute | solution.py:468
  21.2 12.2 %collective-permute-start.3 = (f32[16,1280]{1,0:T(8,128)S(1)}, f32[16,1280]{1,0:T(8,128)S(1)}, u32[]{:S(2)}, u32[]{:S(2)}) collective-permute-start(f32[16,1280]{1,0:T(8,128)S(1)} %get-tuple-element.22), channel_id=1, source_target_pairs={{0,24},{8,0},{16,8},{24,16},{1,25},{9,1},{17,9},{25,17},{2,26},{10... | collective-permute-start | bytes 245768 | tf_op jit(solution)/shard_map/rows/ppermute | solution.py:469
  23.5 2.7 %collective-permute-start.6 = (f32[8,128]{1,0:T(8,128)S(1)}, f32[8,128]{1,0:T(8,128)S(1)}, u32[]{:S(2)}, u32[]{:S(2)}) collective-permute-start(f32[8,128]{1,0:T(8,128)S(1)} %get-tuple-element.25), channel_id=1, source_target_pairs={{0,2},{2,4},{4,6},{6,0},{1,3},{3,5},{5,7},{7,1},{8,10},{10,12},{12... | collective-permute-start | bytes 12296 | tf_op jit(solution)/shard_map/far/ppermute | solution.py:473
  25.5 3.0 %collective-permute-start.7 = (f32[8,128]{1,0:T(8,128)S(1)}, f32[8,128]{1,0:T(8,128)S(1)}, u32[]{:S(2)}, u32[]{:S(2)}) collective-permute-start(f32[8,128]{1,0:T(8,128)S(1)} %get-tuple-element.26), channel_id=1, source_target_pairs={{0,6},{2,0},{4,2},{6,4},{1,7},{3,1},{5,3},{7,5},{8,14},{10,8},{12,... | collective-permute-start | bytes 12296 | tf_op jit(solution)/shard_map/far/ppermute | solution.py:474
  26.3 5.1 %collective-permute-start.4 = (f32[8,2304]{1,0:T(8,128)S(1)}, f32[8,2304]{1,0:T(8,128)S(1)}, u32[]{:S(2)}, u32[]{:S(2)}) collective-permute-start(f32[8,2304]{1,0:T(8,128)S(1)} %get-tuple-element.23), channel_id=1, source_target_pairs={{0,8},{8,16},{16,24},{24,0},{1,9},{9,17},{17,25},{25,1},{2,10},{10... | collective-permute-start | bytes 221192 | tf_op jit(solution)/shard_map/far/ppermute | solution.py:471
  28.6 4.8 %collective-permute-start.5 = (f32[8,2304]{1,0:T(8,128)S(1)}, f32[8,2304]{1,0:T(8,128)S(1)}, u32[]{:S(2)}, u32[]{:S(2)}) collective-permute-start(f32[8,2304]{1,0:T(8,128)S(1)} %get-tuple-element.24), channel_id=1, source_target_pairs={{0,24},{8,0},{16,8},{24,16},{1,25},{9,1},{17,9},{25,17},{2,26},{10... | collective-permute-start | bytes 221192 | tf_op jit(solution)/shard_map/far/ppermute | solution.py:472
  37.6 14.9 %collective-permute-start.10 = (f32[64,1024]{1,0:T(8,128)}, f32[64,1024]{1,0:T(8,128)S(1)}, u32[]{:S(2)}, u32[]{:S(2)}) collective-permute-start(f32[64,1024]{1,0:T(8,128)} %get-tuple-element.16), channel_id=1, source_target_pairs={{0,1},{1,0},{2,3},{3,2},{4,5},{5,4},{6,7},{7,6},{8,9},{9,8},{10,11... | collective-permute-start | bytes 786440 | tf_op jit(solution)/shard_map/height/ppermute | solution.py:493
  39.1 26.7 %collective-permute-start.11 = (f32[64,1024]{1,0:T(8,128)}, f32[64,1024]{1,0:T(8,128)S(1)}, u32[]{:S(2)}, u32[]{:S(2)}) collective-permute-start(f32[64,1024]{1,0:T(8,128)} %get-tuple-element.17), channel_id=1, source_target_pairs={{0,1},{1,0},{2,3},{3,2},{4,5},{5,4},{6,7},{7,6},{8,9},{9,8},{10,11... | collective-permute-start | bytes 786440 | tf_op jit(solution)/shard_map/potential/ppermute | solution.py:495
  39.1 13.3 %collective-permute-start.9 = (f32[8,2048]{1,0:T(8,128)S(1)}, f32[8,2048]{1,0:T(8,128)S(1)}, u32[]{:S(2)}, u32[]{:S(2)}) collective-permute-start(f32[8,2048]{1,0:T(8,128)S(1)} %get-tuple-element.30), channel_id=1, source_target_pairs={{0,1},{1,0},{2,3},{3,2},{4,5},{5,4},{6,7},{7,6},{8,9},{9,8},{10,11... | collective-permute-start | bytes 196616 | tf_op jit(solution)/shard_map/rims/ppermute | solution.py:491
